TPU v7x, 256 devices: a whole 4x4x8 slice. The times are simulated.
256 devices in a mesh: seq: 32 (over y, z), mp: 8 (over x, core).
Axes of the slice: x: 4, y: 4, z: 8, core: 2. Of those that a mesh axis runs over, the one named last changes fastest.
Arguments:
- query_rows: bfloat16 [16384, 8192], P('seq', 'mp'), may hold values from -8 to 8
- key_rows: bfloat16 [16384, 1024], P('seq', 'mp'), may hold values from -8 to 8
- value_rows: bfloat16 [16384, 1024], P('seq', 'mp'), may hold values from -6 to 6
- cotangent: bfloat16 [16384, 8192], P('seq', 'mp'), may hold values from -6 to 6
- router_logits: float32 [16384], P('seq'), may hold values from -8 to 8
- selection: int32 [4096], P('seq'), may hold values from -1 to 511, as said below
Outputs:
- mixed: bfloat16 [16384, 8192], P('seq', 'mp')
- query_grad: bfloat16 [16384, 8192], P('seq', 'mp')
- key_grad: bfloat16 [16384, 1024], P('seq', 'mp')
- value_grad: bfloat16 [16384, 1024], P('seq', 'mp')
- router_grad: float32 [16384], P('seq')
Inputs may be any that keep to these rules, and one draw needn't show every extreme that they name: `selection`: each shard's block of 128 entries lists the local positions of its selected tokens in ascending order, then -1 in the remaining entries; all shards together select exactly 2048 tokens, and some shard selects exactly 128.
All inputs are finite; a program needn't handle non-finite values.
Results may differ from a plain program's by a relative error of at most 0.012.
The roundings to bfloat16 on the way count: a program that leaves them out, or rounds other values in their place, can miss the bound.
Values may be sent and summed in bfloat16 or wider, within the bound.
No kernel may reach another device: no remote copies, remote signals or barrier semaphores. Data moves between devices by JAX's collectives and lax.ppermute only.
A program may use at most 64 MiB of HBM per device.

v0:
```python
import jax
import jax.numpy as jnp
from jax import lax
from jax.sharding import PartitionSpec as P

HEAD_DIM = 128


def place_rows(values_in, targets, tok_rows):
    flat = values_in.reshape(-1, values_in.shape[-1])
    empty = jnp.zeros((tok_rows, flat.shape[-1]), flat.dtype)
    return empty.at[targets.reshape(-1)].set(flat, mode="drop")


def shards(query_rows, key_rows, value_rows, cotangent, router_logits, selection):
    axis_width = lax.axis_size("seq")
    shard_index = lax.axis_index("seq")
    tok_rows = query_rows.shape[0]
    slot_total = selection.shape[0]
    cap_slots = slot_total // axis_width
    block_rows = slot_total // 2
    q_cols = query_rows.shape[1]
    kv_cols = key_rows.shape[1]
    q_heads = q_cols // HEAD_DIM
    kv_heads_dev = kv_cols // HEAD_DIM
    group = q_heads // kv_heads_dev
    scale = HEAD_DIM ** (-0.5)
    picked = selection >= 0
    own_count = jnp.sum(picked.astype(jnp.int32))
    counts = lax.all_gather(own_count.reshape(1), "seq", axis=0, tiled=True)
    offsets = jnp.cumsum(counts) - counts
    lanes = jnp.arange(axis_width, dtype=jnp.int32)
    own_offset = jnp.sum(jnp.where(lanes == shard_index, offsets, 0))
    slot_steps = jnp.arange(cap_slots, dtype=jnp.int32)
    local_index = (
        jnp.mod(lanes - own_offset, axis_width)[:, None] + axis_width * slot_steps[None, :]
    )
    slot_live = local_index < own_count
    positions = jnp.where(slot_live, selection[local_index], tok_rows)
    safe_rows = jnp.minimum(positions, tok_rows - 1)
    live_mask = slot_live[:, :, None]
    router = jax.nn.sigmoid(router_logits[safe_rows])
    cot_rows = cotangent[safe_rows]
    query_send = jnp.where(live_mask, query_rows[safe_rows], 0)
    grad_send = jnp.where(live_mask, router[:, :, None] * cot_rows.astype(jnp.float32), 0.0).astype(
        jnp.bfloat16
    )
    query_recv, grad_recv = (
        lax.all_to_all(query_send, "seq", split_axis=0, concat_axis=0, tiled=True),
        lax.all_to_all(grad_send, "seq", split_axis=0, concat_axis=0, tiled=True),
    )
    row_ids = jnp.arange(block_rows, dtype=jnp.int32)
    query_rank = shard_index + axis_width * row_ids
    shard_ends = offsets + counts
    source = jnp.sum((shard_ends[None, :] <= query_rank[:, None]).astype(jnp.int32), axis=1)
    source_offset = offsets[source]
    first_rank = source_offset + jnp.mod(shard_index - source_offset, axis_width)
    slot_index = source * cap_slots + (query_rank - first_rank) // axis_width

    def compact(received):
        return received.reshape(axis_width * cap_slots, received.shape[2])[slot_index]

    own_rows = jnp.minimum(jnp.where(picked, selection, 0), tok_rows - 1)
    own_pairs = jnp.where(
        picked[:, None], jnp.concatenate([key_rows[own_rows], value_rows[own_rows]], axis=1), 0
    )
    key_set = lax.all_gather(own_pairs, "seq", axis=0, tiled=True)
    key_ids = jnp.arange(axis_width * slot_total, dtype=jnp.int32)
    key_source = key_ids // slot_total
    key_slot = jnp.mod(key_ids, slot_total)
    key_rank = jnp.where(
        key_slot < counts[key_source], offsets[key_source] + key_slot, axis_width * slot_total
    )
    query_block = compact(query_recv)
    grad_block = compact(grad_recv)
    allowed = key_rank[None, :] <= query_rank[:, None]
    contract = (((1,), (1,)), ((), ()))
    weight_list, dscore_list, output_list, dquery_list = ([], [], [], [])
    for head_index in range(q_heads):
        kv_head = head_index // group
        col_start = head_index * HEAD_DIM
        query_head = query_block[:, col_start : col_start + HEAD_DIM]
        grad_head = grad_block[:, col_start : col_start + HEAD_DIM]
        key_head = key_set[:, kv_head * HEAD_DIM : (kv_head + 1) * HEAD_DIM]
        value_head = key_set[:, kv_cols + kv_head * HEAD_DIM : kv_cols + (kv_head + 1) * HEAD_DIM]
        scores = (
            lax.dot_general(query_head, key_head, contract, preferred_element_type=jnp.float32)
            * scale
        )
        top_score = jnp.max(jnp.where(allowed, scores, -jnp.inf), axis=1, keepdims=True)
        expo = jnp.where(allowed, jnp.exp(scores - top_score), 0.0)
        weights = (expo / jnp.sum(expo, axis=1, keepdims=True)).astype(jnp.bfloat16)
        attended = jnp.dot(weights, value_head, preferred_element_type=jnp.float32).astype(
            jnp.bfloat16
        )
        slope = lax.dot_general(grad_head, value_head, contract, preferred_element_type=jnp.float32)
        centre = jnp.sum(
            grad_head.astype(jnp.float32) * attended.astype(jnp.float32), axis=1, keepdims=True
        )
        d_scores = (weights.astype(jnp.float32) * (slope - centre) * scale).astype(jnp.bfloat16)
        dquery_list.append(
            jnp.dot(d_scores, key_head, preferred_element_type=jnp.float32).astype(jnp.bfloat16)
        )
        weight_list.append(weights)
        dscore_list.append(d_scores)
        output_list.append(attended)
    attended_all = jnp.concatenate(output_list, axis=1)
    dquery_all = jnp.concatenate(dquery_list, axis=1)
    key_count = key_set.shape[0]
    weight_stack = jnp.stack(weight_list).reshape(kv_heads_dev, group, block_rows, key_count)
    dscore_stack = jnp.stack(dscore_list).reshape(kv_heads_dev, group, block_rows, key_count)
    query_split = query_block.reshape(block_rows, kv_heads_dev, group, HEAD_DIM)
    grad_split = grad_block.reshape(block_rows, kv_heads_dev, group, HEAD_DIM)
    back_first = offsets + jnp.mod(shard_index - offsets, axis_width)
    back_ranks = back_first[:, None] + axis_width * slot_steps[None, :]
    back_live = (back_ranks < shard_ends[:, None])[:, :, None]
    back_rows = jnp.minimum((back_ranks - shard_index) // axis_width, block_rows - 1)

    def slots_back(rows_in):
        return jnp.where(back_live, rows_in[back_rows], 0)

    key_part = jnp.einsum(
        "hgbk,bhgd->khd", dscore_stack, query_split, preferred_element_type=jnp.float32
    )
    value_part = jnp.einsum(
        "hgbk,bhgd->khd", weight_stack, grad_split, preferred_element_type=jnp.float32
    )
    pair_grads = lax.psum_scatter(
        jnp.concatenate(
            [
                key_part.reshape(lax.axis_size("seq") * slot_total, kv_cols),
                value_part.reshape(lax.axis_size("seq") * slot_total, kv_cols),
            ],
            axis=1,
        ),
        "seq",
        scatter_dimension=0,
        tiled=True,
    ).astype(jnp.bfloat16)
    out_back, dquery_back = (
        lax.all_to_all(slots_back(attended_all), "seq", split_axis=0, concat_axis=0, tiled=True),
        lax.all_to_all(slots_back(dquery_all), "seq", split_axis=0, concat_axis=0, tiled=True),
    )
    own_targets = jnp.where(picked, selection, tok_rows)
    key_grad = place_rows(pair_grads[:, :kv_cols], own_targets, tok_rows)
    value_grad = place_rows(pair_grads[:, kv_cols:], own_targets, tok_rows)
    out_float = out_back.astype(jnp.float32)
    mixed = place_rows((router[:, :, None] * out_float).astype(jnp.bfloat16), positions, tok_rows)
    query_grad = place_rows(dquery_back, positions, tok_rows)
    partial_sums = jnp.sum(cot_rows.astype(jnp.float32) * out_float, axis=2)
    feature_sum = lax.psum(partial_sums, "mp")
    router_terms = (router * (1.0 - router) * feature_sum).reshape(-1)
    router_grad = (
        jnp.zeros((tok_rows,), jnp.float32).at[positions.reshape(-1)].set(router_terms, mode="drop")
    )
    return (mixed, query_grad, key_grad, value_grad, router_grad)


def solution(mesh):
    in_specs = (P("seq", "mp"), P("seq", "mp"), P("seq", "mp"), P("seq", "mp"), P("seq"), P("seq"))
    out_specs = (P("seq", "mp"), P("seq", "mp"), P("seq", "mp"), P("seq", "mp"), P("seq"))
    return jax.shard_map(shards, mesh=mesh, in_specs=in_specs, out_specs=out_specs, check_vma=False)
```

profile of v0, /device:TPU:4, one launch (start us, length us, event | category | flops | bytes accessed | tf_op | source)
XLA Modules:
  0.0 416.3 jit_solution(17175785645465806378)
XLA Ops:
  7.2 1.9 compare_select_fusion.32
  16.4 23.8 %all-reduce = s32[32]{0:T(128)S(1)} all-reduce(s32[32]{0:T(128)S(1)} %dynamic-update-slice), channel_id=1, replica_groups=mesh['seq'=32,'mp'=8] {'seq'}, use_global_device_ids=true, to_apply=%add | all-reduce | flops 32 | bytes 256
  47.1 3.9 all-to-all-start
  54.6 4.4 %compare_select_fusion.21 = s32[4096,1]{0,1:T(1,128)S(1)} fusion(s32[]{:T(128)} %bitcast.62, s32[]{:T(128)} %bitcast.63, s32[]{:T(128)} %bitcast.64, s32[]{:T(128)} %bitcast.65, s32[]{:T(128)} %bitcast.66, s32[]{:T(128)} %bitcast.68, s32[]{:T(128)} %bitcast.67), kind=kLoop, calls=%fused_computation.197 | loop fusion | flops 94208 | bytes 16412 | tf_op jit(solution)/shard_map/gather | solution.py:72
  59.0 4.3 %compare_select_fusion.20 = s32[4096,1]{0,1:T(1,128)S(1)} fusion(s32[]{:T(128)} %bitcast.29, s32[]{:T(128)} %bitcast.30, s32[]{:T(128)} %bitcast.31, s32[]{:T(128)} %bitcast.32, s32[]{:T(128)} %bitcast.33, s32[]{:T(128)} %bitcast.35, s32[]{:T(128)} %bitcast.34), kind=kLoop, calls=%fused_computation.196 | loop fusion | flops 94208 | bytes 16412 | tf_op jit(solution)/shard_map/gather | solution.py:72
  65.3 31.4 %fusion.71 = s32[4096]{0:T(1024)S(1)} fusion(pred[4096]{0:T(1024)(128)(4,1)S(1)} %compare_reduce_fusion, pred[4096]{0:T(1024)(128)(4,1)S(1)} %compare_reduce_fusion.1, pred[4096]{0:T(1024)(128)(4,1)S(1)} %compare_reduce_fusion.2, pred[4096]{0:T(1024)(128)(4,1)S(1)} %compare_reduce_fusion.3, pred[4096]{0:T(1024)(128)(4,1)S(1)} %compare_reduce_fusion.4, ...), kind=kLoop, calls=%fused_computation.239 | loop fusion | flops 241664 | bytes 151752 | tf_op jit(solution)/shard_map/jit(_where)/select_n | solution.py:71
  97.6 1.9 convolution_multiply_fusion.1
  103.7 1.9 fusion.49
  119.2 1.9 broadcast_select_fusion.2
  121.1 9.9 %all-to-all-start.1 = ((bf16[32,4,1024]{2,1,0:T(4,128)(2,1)}), bf16[32,4,1024]{2,1,0:T(4,128)(2,1)}, u32[]{:S(2)}, u32[]{:S(2)}) async-start(bf16[32,4,1024]{2,1,0:T(4,128)(2,1)} %broadcast_select_fusion.2), calls=%async_computation.1 | async-start | bytes 524288 | tf_op jit(solution)/shard_map/all_to_all | solution.py:141
  132.4 3.1 gather_fusion.8
  135.5 1.9 reshape.887
  137.4 4.3 %all-to-all-done.1 = bf16[32,4,1024]{2,1,0:T(4,128)(2,1)} async-done(((bf16[32,4,1024]{2,1,0:T(4,128)(2,1)}), bf16[32,4,1024]{2,1,0:T(4,128)(2,1)}, u32[]{:S(2)}, u32[]{:S(2)}) %all-to-all-start.1) | async-done | bytes 262176 | tf_op jit(solution)/shard_map/all_to_all | solution.py:141
  141.8 2.9 fusion.51
  144.7 5.5 %all-to-all-start.2 = ((bf16[32,4,1024]{2,1,0:T(4,128)(2,1)}), bf16[32,4,1024]{2,1,0:T(4,128)(2,1)}, u32[]{:S(2)}, u32[]{:S(2)}) async-start(bf16[32,4,1024]{2,1,0:T(4,128)(2,1)} %get-tuple-element.50), calls=%async_computation.2 | async-start | bytes 524288 | tf_op jit(solution)/shard_map/all_to_all | solution.py:50
  151.1 9.8 %all-to-all-done.2 = bf16[32,4,1024]{2,1,0:T(4,128)(2,1)} async-done(((bf16[32,4,1024]{2,1,0:T(4,128)(2,1)}), bf16[32,4,1024]{2,1,0:T(4,128)(2,1)}, u32[]{:S(2)}, u32[]{:S(2)}) %all-to-all-start.2) | async-done | bytes 262176 | tf_op jit(solution)/shard_map/all_to_all | solution.py:50
  162.8 4.9 %convolution_bitcast_fusion = f32[4096,128]{0,1:T(8,128)S(1)} fusion(bf16[64,8,128]{2,1,0:T(8,128)(2,1)S(1)} %bitcast.167, bf16[8,64,4096]{2,1,0:T(8,128)(2,1)} %copy-done.4), kind=kOutput, calls=%fused_computation.32 | convolution fusion | flops 536870912 | bytes 6422528 | tf_op jit(solution)/shard_map/hgbk,bhgd->khd/dot_general | solution.py:125
  178.4 2.6 convolution_bitcast_fusion.1
  181.1 2.4 pad_maximum_fusion
  190.4 4.7 %all-to-all-start.3 = ((bf16[32,4,1024]{2,1,0:T(4,128)(2,1)}), bf16[32,4,1024]{2,1,0:T(4,128)(2,1)S(1)}, u32[]{:S(2)}, u32[]{:S(2)}) async-start(bf16[32,4,1024]{2,1,0:T(4,128)(2,1)} %broadcast_select_fusion.1), calls=%async_computation.3 | async-start | bytes 524288 | tf_op jit(solution)/shard_map/all_to_all | solution.py:142
  195.3 20.6 %psum.7 = f32[32,4]{1,0:T(8,128)S(1)} all-reduce(f32[32,4]{1,0:T(8,128)S(1)} %copy-done.31), channel_id=1, replica_groups=mesh['seq'=32,'mp'=8] {'mp'}, use_global_device_ids=true, to_apply=%region_34.35 | all-reduce | flops 128 | bytes 1024 | tf_op jit(solution)/shard_map/psum | solution.py:151
  216.1 2.2 scatter_custom_fusion
  219.9 2.2 scatter_custom_fusion.1
  222.1 183.0 %reduce-scatter.2.cloned.1.call-done = f32[128,256]{0,1:T(8,128)} async-done(((f32[4096,256]{0,1:T(8,128)}), f32[128,256]{0,1:T(8,128)}) %reduce-scatter.2.cloned.1.call-update) | async-done | bytes 131088 | tf_op jit(solution)/shard_map/reduce_scatter | solution.py:128
  (224 shorter events, 66.2 us)
Async XLA Ops:
  7.2 37.2 %copy-start = (bf16[512,1024]{1,0:T(8,128)(2,1)S(1)}, bf16[512,1024]{1,0:T(8,128)(2,1)}, u32[]{:S(2)}) copy-start(bf16[512,1024]{1,0:T(8,128)(2,1)} %param.6) | copy-start | bytes 3145732
  7.2 34.8 %copy-start.1 = (s32[128]{0:T(128)S(1)}, s32[128]{0:T(128)}, u32[]{:S(2)}) copy-start(s32[128]{0:T(128)} %param.11) | copy-start | bytes 1540
  7.2 90.3 %all-gather.2.cloned.1.call-start = ((), (), s32[]{:S(2)}) async-start(), calls=%async_computation.5 | async-start | bytes 2162688 | tf_op jit(solution)/shard_map/all_gather | solution.py:67
  47.1 49.6 %all-to-all-start = ((bf16[32,4,1024]{2,1,0:T(4,128)(2,1)}), bf16[32,4,1024]{2,1,0:T(4,128)(2,1)S(1)}, u32[]{:S(2)}, u32[]{:S(2)}) async-start(bf16[32,4,1024]{2,1,0:T(4,128)(2,1)} %broadcast_select_fusion), calls=%async_computation | async-start | bytes 524288 | tf_op jit(solution)/shard_map/all_to_all | solution.py:49
  107.6 5.5 %copy-start.13 = (bf16[64,4096]{1,0:T(8,128)(2,1)}, bf16[64,4096]{1,0:T(8,128)(2,1)S(1)}, u32[]{:S(2)}) copy-start(bf16[64,4096]{1,0:T(8,128)(2,1)S(1)} %get-tuple-element.34) | copy-start | bytes 1572868
  107.9 6.1 %copy-start.15 = (bf16[64,4096]{1,0:T(8,128)(2,1)}, bf16[64,4096]{1,0:T(8,128)(2,1)S(1)}, u32[]{:S(2)}) copy-start(bf16[64,4096]{1,0:T(8,128)(2,1)S(1)} %get-tuple-element.32) | copy-start | bytes 1572868
  108.2 6.7 %copy-start.17 = (bf16[64,4096]{1,0:T(8,128)(2,1)}, bf16[64,4096]{1,0:T(8,128)(2,1)S(1)}, u32[]{:S(2)}) copy-start(bf16[64,4096]{1,0:T(8,128)(2,1)S(1)} %get-tuple-element.30) | copy-start | bytes 1572868
  115.9 15.1 %copy-start.2 = (f32[512]{0:T(512)S(1)}, f32[512]{0:T(512)}, u32[]{:S(2)}) copy-start(f32[512]{0:T(512)} %param.10) | copy-start | bytes 6148
  121.1 20.7 %all-to-all-start.1 = ((bf16[32,4,1024]{2,1,0:T(4,128)(2,1)}), bf16[32,4,1024]{2,1,0:T(4,128)(2,1)}, u32[]{:S(2)}, u32[]{:S(2)}) async-start(bf16[32,4,1024]{2,1,0:T(4,128)(2,1)} %broadcast_select_fusion.2), calls=%async_computation.1 | async-start | bytes 524288 | tf_op jit(solution)/shard_map/all_to_all | solution.py:141
  132.4 12.3 %copy-start.29 = (f32[32,4]{1,0:T(8,128)}, f32[32,4]{1,0:T(8,128)S(1)}, u32[]{:S(2)}) copy-start(f32[32,4]{1,0:T(8,128)S(1)} %reshape.969) | copy-start | bytes 1540
  144.7 16.3 %all-to-all-start.2 = ((bf16[32,4,1024]{2,1,0:T(4,128)(2,1)}), bf16[32,4,1024]{2,1,0:T(4,128)(2,1)}, u32[]{:S(2)}, u32[]{:S(2)}) async-start(bf16[32,4,1024]{2,1,0:T(4,128)(2,1)} %get-tuple-element.50), calls=%async_computation.2 | async-start | bytes 524288 | tf_op jit(solution)/shard_map/all_to_all | solution.py:50
  150.2 254.9 %reduce-scatter.2.cloned.1.call-start = ((), (), s32[]{:S(2)}) async-start(), calls=%async_computation.6 | async-start | bytes 4325376 | tf_op jit(solution)/shard_map/reduce_scatter | solution.py:128
  162.7 5.0 %copy-start.32 = (bf16[64,128]{1,0:T(8,128)(2,1)S(1)}, bf16[64,128]{1,0:T(8,128)(2,1)}, u32[]{:S(2)}) copy-start(bf16[64,128]{1,0:T(8,128)(2,1)} %get-tuple-element.125) | copy-start | bytes 49156
  162.7 5.0 %copy-start.33 = (bf16[64,128]{1,0:T(8,128)(2,1)S(1)}, bf16[64,128]{1,0:T(8,128)(2,1)}, u32[]{:S(2)}) copy-start(bf16[64,128]{1,0:T(8,128)(2,1)} %get-tuple-element.127) | copy-start | bytes 49156
  162.7 5.0 %copy-start.34 = (bf16[64,128]{1,0:T(8,128)(2,1)S(1)}, bf16[64,128]{1,0:T(8,128)(2,1)}, u32[]{:S(2)}) copy-start(bf16[64,128]{1,0:T(8,128)(2,1)} %get-tuple-element.129) | copy-start | bytes 49156
  162.7 5.0 %copy-start.35 = (bf16[64,128]{1,0:T(8,128)(2,1)S(1)}, bf16[64,128]{1,0:T(8,128)(2,1)}, u32[]{:S(2)}) copy-start(bf16[64,128]{1,0:T(8,128)(2,1)} %get-tuple-element.131) | copy-start | bytes 49156
  162.7 5.0 %copy-start.36 = (bf16[64,128]{1,0:T(8,128)(2,1)S(1)}, bf16[64,128]{1,0:T(8,128)(2,1)}, u32[]{:S(2)}) copy-start(bf16[64,128]{1,0:T(8,128)(2,1)} %get-tuple-element.133) | copy-start | bytes 49156
  162.8 5.0 %copy-start.37 = (bf16[64,128]{1,0:T(8,128)(2,1)S(1)}, bf16[64,128]{1,0:T(8,128)(2,1)}, u32[]{:S(2)}) copy-start(bf16[64,128]{1,0:T(8,128)(2,1)} %get-tuple-element.135) | copy-start | bytes 49156
  162.8 5.0 %copy-start.38 = (bf16[64,128]{1,0:T(8,128)(2,1)S(1)}, bf16[64,128]{1,0:T(8,128)(2,1)}, u32[]{:S(2)}) copy-start(bf16[64,128]{1,0:T(8,128)(2,1)} %get-tuple-element.137) | copy-start | bytes 49156
  162.8 5.2 %copy-start.22 = (bf16[64,4096]{1,0:T(8,128)(2,1)S(1)}, bf16[64,4096]{1,0:T(8,128)(2,1)}, u32[]{:S(2)}) copy-start(bf16[64,4096]{1,0:T(8,128)(2,1)} %copy-done.21) | copy-start | bytes 1572868
  188.5 6.8 %copy-start.19 = (bf16[32,4,1024]{2,1,0:T(4,128)(2,1)S(1)}, bf16[32,4,1024]{2,1,0:T(4,128)(2,1)}, u32[]{:S(2)}) copy-start(bf16[32,4,1024]{2,1,0:T(4,128)(2,1)} %get-tuple-element.51) | copy-start | bytes 786436
  188.5 6.9 %copy-start.31 = (f32[32,4]{1,0:T(8,128)S(1)}, f32[32,4]{1,0:T(8,128)}, u32[]{:S(2)}) copy-start(f32[32,4]{1,0:T(8,128)} %get-tuple-element.49) | copy-start | bytes 1540
  188.5 27.5 %copy-start.30 = (f32[32,4]{1,0:T(8,128)S(1)}, f32[32,4]{1,0:T(8,128)}, u32[]{:S(2)}) copy-start(f32[32,4]{1,0:T(8,128)} %copy-done.29) | copy-start | bytes 1540
  190.4 29.4 %all-to-all-start.3 = ((bf16[32,4,1024]{2,1,0:T(4,128)(2,1)}), bf16[32,4,1024]{2,1,0:T(4,128)(2,1)S(1)}, u32[]{:S(2)}, u32[]{:S(2)}) async-start(bf16[32,4,1024]{2,1,0:T(4,128)(2,1)} %broadcast_select_fusion.1), calls=%async_computation.3 | async-start | bytes 524288 | tf_op jit(solution)/shard_map/all_to_all | solution.py:142
  (22 other events, 59.8 us)
Sparse Core Ops, SparseCore 0:
  13.8 81.9 all-gather.1
  183.6 221.4 reduce-scatter.1
where the time goes:
time: 418 us; the launch traced here: 416 us
  waiting for transfers between devices  197 us (47%)
  other arithmetic  62.7 us (15%)
  blocking collectives  44.4 us (11%)
  local copies, waits for them, and re-layouts  36.6 us (9%)
  matrix products  36.3 us (9%)
  starting transfers between devices  24.2 us (6%)
  between operations  14.9 us (4%)
    reduce_scatter x1, waiting for transfers between devices, shards(): lax.psum_scatter(jnp.concatenate([key_part.reshape(lax.axis_size('seq') *...  183 us
    select_n x1, other arithmetic, shards(): jnp.where(key_slot < counts[key_source], offsets[key_source] + key_slot,...  31.4 us
    unnamed x1, blocking collectives  23.8 us
    psum x1, blocking collectives, shards(): feature_sum = lax.psum(partial_sums, 'mp')  20.6 us
    dot_general x8, matrix products, shards(): lax.dot_general(grad_head, value_head, contract, preferred_element_type=j...  10.3 us
    all_to_all x1, starting transfers between devices, shards(): lax.all_to_all(slots_back(attended_all), 'seq', split_axis=0, concat_axis...  9.92 us
    all_to_all x1, waiting for transfers between devices, shards(): lax.all_to_all(grad_send, 'seq', split_axis=0, concat_axis=0, tiled=True)  9.83 us
  transfers between devices with their start and end apart: 6, of which 3 were waited for; matrix products, arithmetic and copies ran while one was open for 18% of the time, Pallas kernels for 0%

commit v1 on v0

--- a/solution.py
+++ b/solution.py
@@ -148,7 +148,7 @@
     mixed = place_rows((router[:, :, None] * out_float).astype(jnp.bfloat16), positions, tok_rows)
     query_grad = place_rows(dquery_back, positions, tok_rows)
     partial_sums = jnp.sum(cot_rows.astype(jnp.float32) * out_float, axis=2)
-    feature_sum = lax.psum(partial_sums, "mp")
+    feature_sum = jnp.sum(lax.all_gather(partial_sums, "mp"), axis=0)
     router_terms = (router * (1.0 - router) * feature_sum).reshape(-1)
     router_grad = (
         jnp.zeros((tok_rows,), jnp.float32).at[positions.reshape(-1)].set(router_terms, mode="drop")

time: 418 us -> 436 us (1.043)
  waiting for transfers between devices: 197 us -> 219 us
  blocking collectives: 44.4 us -> 35.8 us
    psum x1 -> x0, blocking collectives: 20.6 us -> none  [shards(): feature_sum = lax.psum(partial_sums, 'mp')]
    all_gather x0 -> x1, blocking collectives: none -> 12 us  [shards(): feature_sum = jnp.sum(lax.all_gather(partial_sums, 'mp'), axis=0)]
    reduce_scatter x1, waiting for transfers between devices: 183 us -> 194 us  [shards(): lax.psum_scatter(jnp.concatenate([key_part.reshape(lax.axis_size('seq') *...]
    all_to_all x1, waiting for transfers between devices: 0.01 us -> 8.85 us  [shards(): lax.all_to_all(slots_back(dquery_all), 'seq', split_axis=0, concat_axis=0...]
  transfers between devices with their start and end apart: 6 -> 6, of which waited for: 3 -> 4; matrix products, arithmetic and copies ran while one was open for 18% -> 18% of each run, Pallas kernels for 0% -> 0%
where the time goes in v1:
time: 436 us; the launch traced here: 435 us
  waiting for transfers between devices  219 us (50%)
  other arithmetic  64.4 us (15%)
  local copies, waits for them, and re-layouts  39.6 us (9%)
  matrix products  36.3 us (8%)
  blocking collectives  35.8 us (8%)
  starting transfers between devices  24.3 us (6%)
  between operations  14.9 us (3%)
    reduce_scatter x1, waiting for transfers between devices, shards(): lax.psum_scatter(jnp.concatenate([key_part.reshape(lax.axis_size('seq') *...  194 us
    select_n x1, other arithmetic, shards(): jnp.where(key_slot < counts[key_source], offsets[key_source] + key_slot,...  31.2 us
    unnamed x1, blocking collectives  23.8 us
    all_gather x1, blocking collectives, shards(): feature_sum = jnp.sum(lax.all_gather(partial_sums, 'mp'), axis=0)  12 us
    all_to_all x1, waiting for transfers between devices, shards(): lax.all_to_all(grad_send, 'seq', split_axis=0, concat_axis=0, tiled=True)  11.7 us
    dot_general x8, matrix products, shards(): lax.dot_general(grad_head, value_head, contract, preferred_element_type=j...  10.3 us
    all_to_all x1, starting transfers between devices, shards(): lax.all_to_all(slots_back(attended_all), 'seq', split_axis=0, concat_axis...  9.77 us
    all_to_all x1, waiting for transfers between devices, shards(): lax.all_to_all(slots_back(dquery_all), 'seq', split_axis=0, concat_axis=0...  8.85 us
  transfers between devices with their start and end apart: 6, of which 4 were waited for; matrix products, arithmetic and copies ran while one was open for 18% of the time, Pallas kernels for 0%

profile of v1, /device:TPU:4, one launch (start us, length us, event | category | flops | bytes accessed | tf_op | source)
XLA Modules:
  0.0 434.7 jit_solution(6151515626174869011)
XLA Ops:
  7.2 1.9 compare_select_fusion.32
  16.4 23.8 %all-reduce = s32[32]{0:T(128)S(1)} all-reduce(s32[32]{0:T(128)S(1)} %dynamic-update-slice), channel_id=1, replica_groups=mesh['seq'=32,'mp'=8] {'seq'}, use_global_device_ids=true, to_apply=%add | all-reduce | flops 32 | bytes 256
  47.7 3.9 all-to-all-start
  55.2 4.3 compare_select_fusion.21
  59.5 4.3 compare_select_fusion.20
  66.4 31.2 %fusion.70 = s32[4096]{0:T(1024)S(1)} fusion(pred[4096]{0:T(1024)(128)(4,1)S(1)} %compare_reduce_fusion, pred[4096]{0:T(1024)(128)(4,1)S(1)} %compare_reduce_fusion.1, pred[4096]{0:T(1024)(128)(4,1)S(1)} %compare_reduce_fusion.2, pred[4096]{0:T(1024)(128)(4,1)S(1)} %compare_reduce_fusion.3, pred[4096]{0:T(1024)(128)(4,1)S(1)} %compare_reduce_fusion.4, ...), kind=kLoop, calls=%fused_computation.237 | loop fusion | flops 241664 | bytes 151752 | tf_op jit(solution)/shard_map/jit(_where)/select_n | solution.py:71
  104.5 1.9 fusion.49
  120.3 9.8 %all-to-all-start.1 = ((bf16[32,4,1024]{2,1,0:T(4,128)(2,1)}), bf16[32,4,1024]{2,1,0:T(4,128)(2,1)S(1)}, u32[]{:S(2)}, u32[]{:S(2)}) async-start(bf16[32,4,1024]{2,1,0:T(4,128)(2,1)} %broadcast_select_fusion.2), calls=%async_computation.1 | async-start | bytes 524288 | tf_op jit(solution)/shard_map/all_to_all | solution.py:141
  130.0 3.1 gather_fusion.8
  133.2 1.9 reshape.893
  136.3 4.5 %all-to-all-done.1 = bf16[32,4,1024]{2,1,0:T(4,128)(2,1)S(1)} async-done(((bf16[32,4,1024]{2,1,0:T(4,128)(2,1)}), bf16[32,4,1024]{2,1,0:T(4,128)(2,1)S(1)}, u32[]{:S(2)}, u32[]{:S(2)}) %all-to-all-start.1) | async-done | bytes 262176 | tf_op jit(solution)/shard_map/all_to_all | solution.py:141
  140.8 1.9 fusion.51
  143.5 12.0 %all-gather.1 = f32[8,32,4]{1,2,0:T(4,128)} all-gather(f32[1,32,4]{1,2,0:T(4,128)S(1)} %bitcast.171), channel_id=2, replica_groups=mesh['seq'=32,'mp'=8] {'mp'}, dimensions={0}, use_global_device_ids=true | all-gather | bytes 4608 | tf_op jit(solution)/shard_map/all_gather | solution.py:151
  159.1 2.1 select_convert_fusion
  161.2 5.4 %all-to-all-start.2 = ((bf16[32,4,1024]{2,1,0:T(4,128)(2,1)}), bf16[32,4,1024]{2,1,0:T(4,128)(2,1)}, u32[]{:S(2)}, u32[]{:S(2)}) async-start(bf16[32,4,1024]{2,1,0:T(4,128)(2,1)} %get-tuple-element.53), calls=%async_computation.2 | async-start | bytes 524288 | tf_op jit(solution)/shard_map/all_to_all | solution.py:50
  167.6 11.7 %all-to-all-done.2 = bf16[32,4,1024]{2,1,0:T(4,128)(2,1)} async-done(((bf16[32,4,1024]{2,1,0:T(4,128)(2,1)}), bf16[32,4,1024]{2,1,0:T(4,128)(2,1)}, u32[]{:S(2)}, u32[]{:S(2)}) %all-to-all-start.2) | async-done | bytes 262176 | tf_op jit(solution)/shard_map/all_to_all | solution.py:50
  181.3 4.9 %convolution_bitcast_fusion = f32[4096,128]{0,1:T(8,128)S(1)} fusion(bf16[64,8,128]{2,1,0:T(8,128)(2,1)S(1)} %bitcast.168, bf16[8,64,4096]{2,1,0:T(8,128)(2,1)} %copy-done.4), kind=kOutput, calls=%fused_computation.32 | convolution fusion | flops 536870912 | bytes 6422528 | tf_op jit(solution)/shard_map/hgbk,bhgd->khd/dot_general | solution.py:125
  196.9 2.6 convolution_bitcast_fusion.1
  199.6 2.4 pad_maximum_fusion
  208.9 4.9 %all-to-all-start.3 = ((bf16[32,4,1024]{2,1,0:T(4,128)(2,1)}), bf16[32,4,1024]{2,1,0:T(4,128)(2,1)S(1)}, u32[]{:S(2)}, u32[]{:S(2)}) async-start(bf16[32,4,1024]{2,1,0:T(4,128)(2,1)} %broadcast_select_fusion.1), calls=%async_computation.3 | async-start | bytes 524288 | tf_op jit(solution)/shard_map/all_to_all | solution.py:142
  215.8 2.2 scatter_custom_fusion
  218.0 8.8 %all-to-all-done.3 = bf16[32,4,1024]{2,1,0:T(4,128)(2,1)S(1)} async-done(((bf16[32,4,1024]{2,1,0:T(4,128)(2,1)}), bf16[32,4,1024]{2,1,0:T(4,128)(2,1)S(1)}, u32[]{:S(2)}, u32[]{:S(2)}) %all-to-all-start.3) | async-done | bytes 262176 | tf_op jit(solution)/shard_map/all_to_all | solution.py:142
  226.9 2.2 scatter_custom_fusion.1
  229.1 194.3 %reduce-scatter.2.cloned.1.call-done = f32[128,256]{0,1:T(8,128)} async-done(((f32[4096,256]{0,1:T(8,128)}), f32[128,256]{0,1:T(8,128)}) %reduce-scatter.2.cloned.1.call-update) | async-done | bytes 131088 | tf_op jit(solution)/shard_map/reduce_scatter | solution.py:128
  (231 shorter events, 73.8 us)
Async XLA Ops:
  7.2 37.2 %copy-start = (bf16[512,1024]{1,0:T(8,128)(2,1)S(1)}, bf16[512,1024]{1,0:T(8,128)(2,1)}, u32[]{:S(2)}) copy-start(bf16[512,1024]{1,0:T(8,128)(2,1)} %param.6) | copy-start | bytes 3145732
  7.2 34.8 %copy-start.1 = (s32[128]{0:T(128)S(1)}, s32[128]{0:T(128)}, u32[]{:S(2)}) copy-start(s32[128]{0:T(128)} %param.11) | copy-start | bytes 1540
  7.2 91.2 %all-gather.4.cloned.1.call-start = ((), (), s32[]{:S(2)}) async-start(), calls=%async_computation.5 | async-start | bytes 2162688 | tf_op jit(solution)/shard_map/all_gather | solution.py:67
  46.8 8.4 %copy-start.31 = (pred[32,4]{1,0:T(8,128)(4,1)}, pred[32,4]{1,0:T(8,128)(4,1)S(1)}, u32[]{:S(2)}) copy-start(pred[32,4]{1,0:T(8,128)(4,1)S(1)} %copy.37) | copy-start | bytes 388
  47.7 49.9 %all-to-all-start = ((bf16[32,4,1024]{2,1,0:T(4,128)(2,1)}), bf16[32,4,1024]{2,1,0:T(4,128)(2,1)S(1)}, u32[]{:S(2)}, u32[]{:S(2)}) async-start(bf16[32,4,1024]{2,1,0:T(4,128)(2,1)} %broadcast_select_fusion), calls=%async_computation | async-start | bytes 524288 | tf_op jit(solution)/shard_map/all_to_all | solution.py:49
  53.7 46.6 %copy-start.41 = (s32[1024]{0:T(1024)}, s32[1024]{0:T(1024)S(1)}, u32[]{:S(2)}) copy-start(s32[1024]{0:T(1024)S(1)} %pad_clamp_fusion.2) | copy-start | bytes 12292
  108.4 5.5 %copy-start.13 = (bf16[64,4096]{1,0:T(8,128)(2,1)}, bf16[64,4096]{1,0:T(8,128)(2,1)S(1)}, u32[]{:S(2)}) copy-start(bf16[64,4096]{1,0:T(8,128)(2,1)S(1)} %get-tuple-element.36) | copy-start | bytes 1572868
  108.7 6.1 %copy-start.15 = (bf16[64,4096]{1,0:T(8,128)(2,1)}, bf16[64,4096]{1,0:T(8,128)(2,1)S(1)}, u32[]{:S(2)}) copy-start(bf16[64,4096]{1,0:T(8,128)(2,1)S(1)} %get-tuple-element.34) | copy-start | bytes 1572868
  109.1 6.7 %copy-start.17 = (bf16[64,4096]{1,0:T(8,128)(2,1)}, bf16[64,4096]{1,0:T(8,128)(2,1)S(1)}, u32[]{:S(2)}) copy-start(bf16[64,4096]{1,0:T(8,128)(2,1)S(1)} %get-tuple-element.32) | copy-start | bytes 1572868
  119.3 15.7 %copy-start.2 = (f32[512]{0:T(512)S(1)}, f32[512]{0:T(512)}, u32[]{:S(2)}) copy-start(f32[512]{0:T(512)} %param.10) | copy-start | bytes 6148
  120.3 20.6 %all-to-all-start.1 = ((bf16[32,4,1024]{2,1,0:T(4,128)(2,1)}), bf16[32,4,1024]{2,1,0:T(4,128)(2,1)S(1)}, u32[]{:S(2)}, u32[]{:S(2)}) async-start(bf16[32,4,1024]{2,1,0:T(4,128)(2,1)} %broadcast_select_fusion.2), calls=%async_computation.1 | async-start | bytes 524288 | tf_op jit(solution)/shard_map/all_to_all | solution.py:141
  161.2 18.1 %all-to-all-start.2 = ((bf16[32,4,1024]{2,1,0:T(4,128)(2,1)}), bf16[32,4,1024]{2,1,0:T(4,128)(2,1)}, u32[]{:S(2)}, u32[]{:S(2)}) async-start(bf16[32,4,1024]{2,1,0:T(4,128)(2,1)} %get-tuple-element.53), calls=%async_computation.2 | async-start | bytes 524288 | tf_op jit(solution)/shard_map/all_to_all | solution.py:50
  166.6 256.8 %reduce-scatter.2.cloned.1.call-start = ((), (), s32[]{:S(2)}) async-start(), calls=%async_computation.6 | async-start | bytes 4325376 | tf_op jit(solution)/shard_map/reduce_scatter | solution.py:128
  181.2 5.0 %copy-start.32 = (bf16[64,128]{1,0:T(8,128)(2,1)S(1)}, bf16[64,128]{1,0:T(8,128)(2,1)}, u32[]{:S(2)}) copy-start(bf16[64,128]{1,0:T(8,128)(2,1)} %get-tuple-element.126) | copy-start | bytes 49156
  181.2 5.0 %copy-start.33 = (bf16[64,128]{1,0:T(8,128)(2,1)S(1)}, bf16[64,128]{1,0:T(8,128)(2,1)}, u32[]{:S(2)}) copy-start(bf16[64,128]{1,0:T(8,128)(2,1)} %get-tuple-element.128) | copy-start | bytes 49156
  181.2 5.0 %copy-start.34 = (bf16[64,128]{1,0:T(8,128)(2,1)S(1)}, bf16[64,128]{1,0:T(8,128)(2,1)}, u32[]{:S(2)}) copy-start(bf16[64,128]{1,0:T(8,128)(2,1)} %get-tuple-element.130) | copy-start | bytes 49156
  181.2 5.0 %copy-start.35 = (bf16[64,128]{1,0:T(8,128)(2,1)S(1)}, bf16[64,128]{1,0:T(8,128)(2,1)}, u32[]{:S(2)}) copy-start(bf16[64,128]{1,0:T(8,128)(2,1)} %get-tuple-element.132) | copy-start | bytes 49156
  181.2 5.0 %copy-start.36 = (bf16[64,128]{1,0:T(8,128)(2,1)S(1)}, bf16[64,128]{1,0:T(8,128)(2,1)}, u32[]{:S(2)}) copy-start(bf16[64,128]{1,0:T(8,128)(2,1)} %get-tuple-element.134) | copy-start | bytes 49156
  181.2 5.0 %copy-start.37 = (bf16[64,128]{1,0:T(8,128)(2,1)S(1)}, bf16[64,128]{1,0:T(8,128)(2,1)}, u32[]{:S(2)}) copy-start(bf16[64,128]{1,0:T(8,128)(2,1)} %get-tuple-element.136) | copy-start | bytes 49156
  181.2 5.0 %copy-start.38 = (bf16[64,128]{1,0:T(8,128)(2,1)S(1)}, bf16[64,128]{1,0:T(8,128)(2,1)}, u32[]{:S(2)}) copy-start(bf16[64,128]{1,0:T(8,128)(2,1)} %get-tuple-element.138) | copy-start | bytes 49156
  181.3 5.2 %copy-start.22 = (bf16[64,4096]{1,0:T(8,128)(2,1)S(1)}, bf16[64,4096]{1,0:T(8,128)(2,1)}, u32[]{:S(2)}) copy-start(bf16[64,4096]{1,0:T(8,128)(2,1)} %copy-done.21) | copy-start | bytes 1572868
  207.0 6.8 %copy-start.40 = (s32[32,4]{0,1:T(4,128)S(1)}, s32[32,4]{0,1:T(4,128)}, u32[]{:S(2)}) copy-start(s32[32,4]{0,1:T(4,128)} %get-tuple-element.49) | copy-start | bytes 1540
  207.0 7.0 %copy-start.19 = (bf16[32,4,1024]{2,1,0:T(4,128)(2,1)S(1)}, bf16[32,4,1024]{2,1,0:T(4,128)(2,1)}, u32[]{:S(2)}) copy-start(bf16[32,4,1024]{2,1,0:T(4,128)(2,1)} %get-tuple-element.54) | copy-start | bytes 786436
  208.9 17.9 %all-to-all-start.3 = ((bf16[32,4,1024]{2,1,0:T(4,128)(2,1)}), bf16[32,4,1024]{2,1,0:T(4,128)(2,1)S(1)}, u32[]{:S(2)}, u32[]{:S(2)}) async-start(bf16[32,4,1024]{2,1,0:T(4,128)(2,1)} %broadcast_select_fusion.1), calls=%async_computation.3 | async-start | bytes 524288 | tf_op jit(solution)/shard_map/all_to_all | solution.py:142
  (24 other events, 64.8 us)
Sparse Core Ops, SparseCore 0:
  13.8 81.0 all-gather.3
  202.1 221.2 reduce-scatter.1
